TPU v7x, 512 devices: a whole 4x4x16 slice. The times are simulated.
512 devices in a mesh: ctx: 64 (over x, z_lo, y), tp: 8 (over z_hi, core).
Axes of the slice: x: 4, y: 4, z: 16 (z_hi: 4, z_lo: 4; z = z_hi * 4 + z_lo), core: 2. Of those that a mesh axis runs over, the one named last changes fastest.
Arguments:
- layer_cotangent: bfloat16 [16384, 5376], P('ctx', 'tp'), may hold values from -6 to 6
- out_weight: bfloat16 [2048, 5376], P(None, 'tp'), may hold values from -0.078125 to 0.078125
- queries: bfloat16 [16384, 2048], P('ctx', 'tp'), may hold values from -38 to 38
- keys: bfloat16 [16384, 1024], P('ctx', 'tp'), may hold values from -13 to 13
- values: bfloat16 [16384, 1024], P('ctx', 'tp'), may hold values from -6 to 6
Outputs:
- query_grads: bfloat16 [16384, 2048], P('ctx', 'tp')
- key_gradients: bfloat16 [16384, 1024], P('ctx', 'tp')
- value_gradients: bfloat16 [16384, 1024], P('ctx', 'tp')
All inputs are finite; a program needn't handle non-finite values.
Results may differ from a plain program's by a relative error of at most 0.03.
Values may be sent and summed in bfloat16 or wider, within the bound.
A program may use at most 64 MiB of HBM per device.

v0:
```python
import jax
import jax.numpy as jnp
from jax import lax
from jax.sharding import PartitionSpec as P

HEAD_SIZE = 128
WINDOW_LENGTH = 1024


score_scale = 168.0 ** (-0.5)


def shifted(value, axis, steps):
    count = lax.axis_size(axis)
    leading, last = (max(0, -steps), min(count, count - steps))
    return lax.ppermute(value, axis, [(source, source + steps) for source in range(leading, last)])


def local(layer_cotangent, out_weight, queries, keys, values):
    tokens_here = queries.shape[0]
    query_heads = queries.shape[1] // HEAD_SIZE
    kv_heads = keys.shape[1] // HEAD_SIZE
    query_group = query_heads // kv_heads
    blocks_back = WINDOW_LENGTH // tokens_here
    head_rows = query_heads * HEAD_SIZE
    grads_turned = lax.psum_scatter(
        lax.dot_general(
            out_weight,
            layer_cotangent,
            (((1,), (1,)), ((), ())),
            preferred_element_type=jnp.float32,
        ).astype(jnp.bfloat16),
        "tp",
        scatter_dimension=0,
        tiled=True,
    )
    earlier = []
    for offset in range(blocks_back):
        earlier.append(shifted((keys, values), "ctx", offset + 1))
    key_whole = jnp.concatenate(
        [earlier[blocks_back - 1 - number][0] for number in range(blocks_back)] + [keys], axis=0
    )
    value_whole = jnp.concatenate(
        [earlier[blocks_back - 1 - number][1] for number in range(blocks_back)] + [values], axis=0
    )
    key_whole = key_whole.reshape(WINDOW_LENGTH + tokens_here, kv_heads, HEAD_SIZE)
    value_whole = value_whole.reshape(WINDOW_LENGTH + tokens_here, kv_heads, HEAD_SIZE)
    query_quad = queries.reshape(tokens_here, kv_heads, query_group, HEAD_SIZE)
    grads_four = grads_turned.reshape(kv_heads, query_group, HEAD_SIZE, tokens_here)
    base_pos = lax.axis_index("ctx") * tokens_here - WINDOW_LENGTH
    block = min(tokens_here, 512)
    key_total = jnp.zeros((WINDOW_LENGTH + tokens_here, kv_heads, HEAD_SIZE), jnp.float32)
    value_total = jnp.zeros((WINDOW_LENGTH + tokens_here, kv_heads, HEAD_SIZE), jnp.float32)
    row_ids = jnp.arange(block, dtype=jnp.int32)[:, None]
    col_ids = jnp.arange(block + WINDOW_LENGTH, dtype=jnp.int32)[None, :]
    reach = col_ids - row_ids
    visible = (reach >= 1) & (reach <= WINDOW_LENGTH) & (base_pos + 0 + col_ids >= 0)
    scores = (
        jnp.einsum("qhgd,khd->hgqk", query_quad, key_whole, preferred_element_type=jnp.float32)
        * score_scale
    )
    scores = jnp.where(visible, scores, -jnp.inf)
    top = jnp.max(scores, axis=-1, keepdims=True)
    expo = jnp.exp(scores - top)
    probs = expo / jnp.sum(expo, axis=-1, keepdims=True)
    probs_low = probs.astype(jnp.bfloat16)
    dprobs = jnp.einsum(
        "hgdq,khd->hgqk", grads_four, value_whole, preferred_element_type=jnp.float32
    )
    delta = jnp.sum(probs * dprobs, axis=-1, keepdims=True)
    dscores = (probs * (dprobs - delta) * score_scale).astype(jnp.bfloat16)
    query_part = jnp.einsum(
        "hgqk,khd->qhgd", dscores, key_whole, preferred_element_type=jnp.float32
    )
    query_pieces = query_part.astype(jnp.bfloat16).reshape(block, head_rows)
    key_part = jnp.einsum("hgqk,qhgd->khd", dscores, query_quad, preferred_element_type=jnp.float32)
    value_part = jnp.einsum(
        "hgqk,hgdq->khd", probs_low, grads_four, preferred_element_type=jnp.float32
    )
    key_total = key_total.at[0 : block + WINDOW_LENGTH].add(key_part)
    value_total = value_total.at[0 : block + WINDOW_LENGTH].add(value_part)
    flat_width = kv_heads * HEAD_SIZE
    key_sum = key_total[WINDOW_LENGTH:].reshape(tokens_here, flat_width)
    value_sum = value_total[WINDOW_LENGTH:].reshape(tokens_here, flat_width)
    key_parts = []
    value_parts = []
    for offset in range(1, blocks_back + 1):
        lower = WINDOW_LENGTH - offset * tokens_here
        key_parts.append(
            key_total[lower : lower + tokens_here]
            .reshape(tokens_here, flat_width)
            .astype(jnp.bfloat16)
        )
        value_parts.append(
            value_total[lower : lower + tokens_here]
            .reshape(tokens_here, flat_width)
            .astype(jnp.bfloat16)
        )
    for offset in range(1, blocks_back + 1):
        arrived = shifted((key_parts[offset - 1], value_parts[offset - 1]), "ctx", -offset)
        key_sum = key_sum + arrived[0].astype(jnp.float32)
        value_sum = value_sum + arrived[1].astype(jnp.float32)
    return (query_pieces, key_sum.astype(jnp.bfloat16), value_sum.astype(jnp.bfloat16))


def solution(mesh):
    in_specs = (P("ctx", "tp"), P(None, "tp"), P("ctx", "tp"), P("ctx", "tp"), P("ctx", "tp"))
    out_specs = (P("ctx", "tp"), P("ctx", "tp"), P("ctx", "tp"))
    return jax.shard_map(local, mesh=mesh, in_specs=in_specs, out_specs=out_specs, check_vma=False)
```

profile of v0, /device:TPU:26, one launch (start us, length us, event | category | flops | bytes accessed | tf_op | source)
XLA Modules:
  0.0 140.0 jit_solution(12176015568711101947)
XLA Ops:
  7.2 4.8 %collective-permute-start.2 = (bf16[256,128]{1,0:T(8,128)(2,1)}, bf16[256,128]{1,0:T(8,128)(2,1)S(1)}, u32[]{:S(2)}, u32[]{:S(2)}) collective-permute-start(bf16[256,128]{1,0:T(8,128)(2,1)} %param.16), channel_id=1, source_target_pairs={{0,16},{8,24},{16,32},{24,40},{32,48},{40,56},{48,64},{56,72},{64,... | collective-permute-start | bytes 196616 | tf_op jit(solution)/shard_map/ppermute | solution.py:16
  12.0 3.1 %collective-permute-start.1 = (bf16[256,128]{1,0:T(8,128)(2,1)}, bf16[256,128]{1,0:T(8,128)(2,1)S(1)}, u32[]{:S(2)}, u32[]{:S(2)}) collective-permute-start(bf16[256,128]{1,0:T(8,128)(2,1)} %param.16), channel_id=1, source_target_pairs={{0,24},{8,32},{16,40},{24,48},{32,56},{40,64},{48,72},{56,80},{64,... | collective-permute-start | bytes 196616 | tf_op jit(solution)/shard_map/ppermute | solution.py:16
  15.1 3.8 %collective-permute-start = (bf16[256,128]{1,0:T(8,128)(2,1)}, bf16[256,128]{1,0:T(8,128)(2,1)S(1)}, u32[]{:S(2)}, u32[]{:S(2)}) collective-permute-start(bf16[256,128]{1,0:T(8,128)(2,1)} %param.16), channel_id=1, source_target_pairs={{0,32},{8,40},{16,48},{24,56},{32,64},{40,72},{48,80},{56,88},{64,... | collective-permute-start | bytes 196616 | tf_op jit(solution)/shard_map/ppermute | solution.py:16
  19.0 5.3 %collective-permute-start.3 = (bf16[256,128]{1,0:T(8,128)(2,1)}, bf16[256,128]{1,0:T(8,128)(2,1)S(1)}, u32[]{:S(2)}, u32[]{:S(2)}) collective-permute-start(bf16[256,128]{1,0:T(8,128)(2,1)} %param.16), channel_id=1, source_target_pairs={{0,8},{8,16},{16,24},{24,32},{32,40},{40,48},{48,56},{56,64},{64,7... | collective-permute-start | bytes 196616 | tf_op jit(solution)/shard_map/ppermute | solution.py:16
  24.3 2.0 %collective-permute-start.4 = (bf16[256,128]{1,0:T(8,128)(2,1)}, bf16[256,128]{1,0:T(8,128)(2,1)S(1)}, u32[]{:S(2)}, u32[]{:S(2)}) collective-permute-start(bf16[256,128]{1,0:T(8,128)(2,1)} %param.17), channel_id=1, source_target_pairs={{0,32},{8,40},{16,48},{24,56},{32,64},{40,72},{48,80},{56,88},{64,... | collective-permute-start | bytes 196616 | tf_op jit(solution)/shard_map/ppermute | solution.py:16
  26.3 3.0 %convolution_convert_fusion = bf16[2048,256]{1,0:T(8,128)(2,1)} fusion(bf16[2048,672]{0,1:T(8,128)(2,1)S(1)} %copy-done, bf16[256,672]{0,1:T(8,128)(2,1)} %param.13), kind=kOutput, calls=%fused_computation.9 | convolution fusion | flops 705167360 | bytes 4145152 | tf_op jit(solution)/shard_map/dot_general | solution.py:27
  29.6 3.7 %collective-permute-done.4 = bf16[256,128]{1,0:T(8,128)(2,1)S(1)} collective-permute-done((bf16[256,128]{1,0:T(8,128)(2,1)}, bf16[256,128]{1,0:T(8,128)(2,1)S(1)}, u32[]{:S(2)}, u32[]{:S(2)}) %collective-permute-start.4) | collective-permute-done | bytes 65568 | tf_op jit(solution)/shard_map/ppermute | solution.py:16
  33.3 1.9 %collective-permute-start.5 = (bf16[256,128]{1,0:T(8,128)(2,1)S(1)}, bf16[256,128]{1,0:T(8,128)(2,1)S(1)}, u32[]{:S(2)}, u32[]{:S(2)}) collective-permute-start(bf16[256,128]{1,0:T(8,128)(2,1)S(1)} %copy-done.5), channel_id=1, source_target_pairs={{0,24},{8,32},{16,40},{24,48},{32,56},{40,64},{48,72},{56,80},{64,... | collective-permute-start | bytes 196616 | tf_op jit(solution)/shard_map/ppermute | solution.py:16
  35.3 5.4 %collective-permute-done.5 = bf16[256,128]{1,0:T(8,128)(2,1)S(1)} collective-permute-done((bf16[256,128]{1,0:T(8,128)(2,1)S(1)}, bf16[256,128]{1,0:T(8,128)(2,1)S(1)}, u32[]{:S(2)}, u32[]{:S(2)}) %collective-permute-start.5) | collective-permute-done | bytes 65568 | tf_op jit(solution)/shard_map/ppermute | solution.py:16
  40.7 1.9 %collective-permute-start.6 = (bf16[256,128]{1,0:T(8,128)(2,1)S(1)}, bf16[256,128]{1,0:T(8,128)(2,1)S(1)}, u32[]{:S(2)}, u32[]{:S(2)}) collective-permute-start(bf16[256,128]{1,0:T(8,128)(2,1)S(1)} %copy-done.5), channel_id=1, source_target_pairs={{0,16},{8,24},{16,32},{24,40},{32,48},{40,56},{48,64},{56,72},{64,... | collective-permute-start | bytes 196616 | tf_op jit(solution)/shard_map/ppermute | solution.py:16
  42.6 5.7 %collective-permute-done.6 = bf16[256,128]{1,0:T(8,128)(2,1)S(1)} collective-permute-done((bf16[256,128]{1,0:T(8,128)(2,1)S(1)}, bf16[256,128]{1,0:T(8,128)(2,1)S(1)}, u32[]{:S(2)}, u32[]{:S(2)}) %collective-permute-start.6) | collective-permute-done | bytes 65568 | tf_op jit(solution)/shard_map/ppermute | solution.py:16
  48.4 3.0 %collective-permute-start.7 = (bf16[256,128]{1,0:T(8,128)(2,1)S(1)}, bf16[256,128]{1,0:T(8,128)(2,1)S(1)}, u32[]{:S(2)}, u32[]{:S(2)}) collective-permute-start(bf16[256,128]{1,0:T(8,128)(2,1)S(1)} %copy-done.5), channel_id=1, source_target_pairs={{0,8},{8,16},{16,24},{24,32},{32,40},{40,48},{48,56},{56,64},{64,7... | collective-permute-start | bytes 196616 | tf_op jit(solution)/shard_map/ppermute | solution.py:16
  51.4 3.1 %collective-permute-done.7 = bf16[256,128]{1,0:T(8,128)(2,1)S(1)} collective-permute-done((bf16[256,128]{1,0:T(8,128)(2,1)S(1)}, bf16[256,128]{1,0:T(8,128)(2,1)S(1)}, u32[]{:S(2)}, u32[]{:S(2)}) %collective-permute-start.7) | collective-permute-done | bytes 65568 | tf_op jit(solution)/shard_map/ppermute | solution.py:16
  57.7 29.9 %reduce-scatter.2.cloned.1.call-done = bf16[256,256]{1,0:T(8,128)(2,1)} async-done(((bf16[2048,256]{1,0:T(8,128)(2,1)}), bf16[256,256]{1,0:T(8,128)(2,1)}) %reduce-scatter.2.cloned.1.call-update) | async-done | bytes 131088 | tf_op jit(solution)/shard_map/reduce_scatter | solution.py:26
  87.6 3.4 %fusion.35 = (bf16[1280,1,128]{0,2,1:T(8,128)(2,1)S(1)}, f32[1280,1,128]{0,2,1:T(8,128)}) fusion(bf16[2,128,256]{2,1,0:T(8,128)(2,1)} %bitcast.120, f32[2,256]{1,0:T(2,128)S(1)} %fusion.6, f32[1,2,256,1280]{2,3,1,0:T(8,128)} %copy-done.1, f32[2,256]{1,0:T(2,128)S(1)} %get-tuple-element.54), kind=kOutput, calls=%fused_computation.64 | convolution fusion | flops 169902080 | bytes 3739648 | tf_op jit(solution)/shard_map/hgqk,hgdq->khd/dot_general | solution.py:77
  93.9 2.2 %collective-permute-start.12 = (bf16[256,128]{0,1:T(8,128)(2,1)}, bf16[256,128]{0,1:T(8,128)(2,1)}, u32[]{:S(2)}, u32[]{:S(2)}) collective-permute-start(bf16[256,128]{0,1:T(8,128)(2,1)} %get-tuple-element.46), channel_id=1, source_target_pairs={{8,0},{16,8},{24,16},{32,24},{40,32},{48,40},{56,48},{64,56},{72,6... | collective-permute-start | bytes 196616 | tf_op jit(solution)/shard_map/ppermute | solution.py:16
  96.1 4.8 %collective-permute-start.15 = (bf16[256,128]{0,1:T(8,128)(2,1)}, bf16[256,128]{0,1:T(8,128)(2,1)}, u32[]{:S(2)}, u32[]{:S(2)}) collective-permute-start(bf16[256,128]{0,1:T(8,128)(2,1)} %get-tuple-element.47), channel_id=1, source_target_pairs={{32,0},{40,8},{48,16},{56,24},{64,32},{72,40},{80,48},{88,56},{96,... | collective-permute-start | bytes 196616 | tf_op jit(solution)/shard_map/ppermute | solution.py:16
  100.9 5.2 %collective-permute-start.14 = (bf16[256,128]{0,1:T(8,128)(2,1)}, bf16[256,128]{0,1:T(8,128)(2,1)}, u32[]{:S(2)}, u32[]{:S(2)}) collective-permute-start(bf16[256,128]{0,1:T(8,128)(2,1)} %get-tuple-element.48), channel_id=1, source_target_pairs={{24,0},{32,8},{40,16},{48,24},{56,32},{64,40},{72,48},{80,56},{88,... | collective-permute-start | bytes 196616 | tf_op jit(solution)/shard_map/ppermute | solution.py:16
  106.1 1.9 %collective-permute-start.13 = (bf16[256,128]{0,1:T(8,128)(2,1)}, bf16[256,128]{0,1:T(8,128)(2,1)}, u32[]{:S(2)}, u32[]{:S(2)}) collective-permute-start(bf16[256,128]{0,1:T(8,128)(2,1)} %get-tuple-element.49), channel_id=1, source_target_pairs={{16,0},{24,8},{32,16},{40,24},{48,32},{56,40},{64,48},{72,56},{80,... | collective-permute-start | bytes 196616 | tf_op jit(solution)/shard_map/ppermute | solution.py:16
  109.5 2.8 %collective-permute-start.8 = (bf16[256,128]{1,0:T(8,128)(2,1)}, bf16[256,128]{1,0:T(8,128)(2,1)S(1)}, u32[]{:S(2)}, u32[]{:S(2)}) collective-permute-start(bf16[256,128]{1,0:T(8,128)(2,1)} %get-tuple-element.50), channel_id=1, source_target_pairs={{8,0},{16,8},{24,16},{32,24},{40,32},{48,40},{56,48},{64,56},{72,6... | collective-permute-start | bytes 196616 | tf_op jit(solution)/shard_map/ppermute | solution.py:16
  112.4 1.9 %collective-permute-start.11 = (bf16[256,128]{1,0:T(8,128)(2,1)}, bf16[256,128]{1,0:T(8,128)(2,1)}, u32[]{:S(2)}, u32[]{:S(2)}) collective-permute-start(bf16[256,128]{1,0:T(8,128)(2,1)} %get-tuple-element.51), channel_id=1, source_target_pairs={{32,0},{40,8},{48,16},{56,24},{64,32},{72,40},{80,48},{88,56},{96,... | collective-permute-start | bytes 196616 | tf_op jit(solution)/shard_map/ppermute | solution.py:16
  114.3 8.3 %collective-permute-start.10 = (bf16[256,128]{1,0:T(8,128)(2,1)}, bf16[256,128]{1,0:T(8,128)(2,1)}, u32[]{:S(2)}, u32[]{:S(2)}) collective-permute-start(bf16[256,128]{1,0:T(8,128)(2,1)} %get-tuple-element.52), channel_id=1, source_target_pairs={{24,0},{32,8},{40,16},{48,24},{56,32},{64,40},{72,48},{80,56},{88,... | collective-permute-start | bytes 196616 | tf_op jit(solution)/shard_map/ppermute | solution.py:16
  122.7 1.9 %collective-permute-start.9 = (bf16[256,128]{1,0:T(8,128)(2,1)}, bf16[256,128]{1,0:T(8,128)(2,1)}, u32[]{:S(2)}, u32[]{:S(2)}) collective-permute-start(bf16[256,128]{1,0:T(8,128)(2,1)} %get-tuple-element.53), channel_id=1, source_target_pairs={{16,0},{24,8},{32,16},{40,24},{48,32},{56,40},{64,48},{72,56},{80,... | collective-permute-start | bytes 196616 | tf_op jit(solution)/shard_map/ppermute | solution.py:16
  126.4 5.1 %collective-permute-done.9 = bf16[256,128]{1,0:T(8,128)(2,1)} collective-permute-done((bf16[256,128]{1,0:T(8,128)(2,1)}, bf16[256,128]{1,0:T(8,128)(2,1)}, u32[]{:S(2)}, u32[]{:S(2)}) %collective-permute-start.9) | collective-permute-done | bytes 65568 | tf_op jit(solution)/shard_map/ppermute | solution.py:16
  (57 shorter events, 11.2 us)
Async XLA Ops:
  7.2 19.1 %copy-start = (bf16[2048,672]{0,1:T(8,128)(2,1)S(1)}, bf16[2048,672]{0,1:T(8,128)(2,1)}, u32[]{:S(2)}) copy-start(bf16[2048,672]{0,1:T(8,128)(2,1)} %param.14) | copy-start | bytes 8257540
  7.2 48.1 %copy-start.6 = (bf16[256,128]{1,0:T(8,128)(2,1)S(1)}, bf16[256,128]{1,0:T(8,128)(2,1)}, u32[]{:S(2)}) copy-start(bf16[256,128]{1,0:T(8,128)(2,1)} %param.16) | copy-start | bytes 196612
  7.2 26.1 %copy-start.5 = (bf16[256,128]{1,0:T(8,128)(2,1)S(1)}, bf16[256,128]{1,0:T(8,128)(2,1)}, u32[]{:S(2)}) copy-start(bf16[256,128]{1,0:T(8,128)(2,1)} %param.17) | copy-start | bytes 196612
  7.2 80.3 %reduce-scatter.2.cloned.1.call-start = ((), (), s32[]{:S(2)}) async-start(), calls=%async_computation.1 | async-start | bytes 1179648 | tf_op jit(solution)/shard_map/reduce_scatter | solution.py:26
  7.2 47.4 %collective-permute-start.2 = (bf16[256,128]{1,0:T(8,128)(2,1)}, bf16[256,128]{1,0:T(8,128)(2,1)S(1)}, u32[]{:S(2)}, u32[]{:S(2)}) collective-permute-start(bf16[256,128]{1,0:T(8,128)(2,1)} %param.16), channel_id=1, source_target_pairs={{0,16},{8,24},{16,32},{24,40},{32,48},{40,56},{48,64},{56,72},{64,... | collective-permute-start | bytes 196616 | tf_op jit(solution)/shard_map/ppermute | solution.py:16
  12.0 42.6 %collective-permute-start.1 = (bf16[256,128]{1,0:T(8,128)(2,1)}, bf16[256,128]{1,0:T(8,128)(2,1)S(1)}, u32[]{:S(2)}, u32[]{:S(2)}) collective-permute-start(bf16[256,128]{1,0:T(8,128)(2,1)} %param.16), channel_id=1, source_target_pairs={{0,24},{8,32},{16,40},{24,48},{32,56},{40,64},{48,72},{56,80},{64,... | collective-permute-start | bytes 196616 | tf_op jit(solution)/shard_map/ppermute | solution.py:16
  15.1 39.4 %collective-permute-start = (bf16[256,128]{1,0:T(8,128)(2,1)}, bf16[256,128]{1,0:T(8,128)(2,1)S(1)}, u32[]{:S(2)}, u32[]{:S(2)}) collective-permute-start(bf16[256,128]{1,0:T(8,128)(2,1)} %param.16), channel_id=1, source_target_pairs={{0,32},{8,40},{16,48},{24,56},{32,64},{40,72},{48,80},{56,88},{64,... | collective-permute-start | bytes 196616 | tf_op jit(solution)/shard_map/ppermute | solution.py:16
  19.0 35.7 %collective-permute-start.3 = (bf16[256,128]{1,0:T(8,128)(2,1)}, bf16[256,128]{1,0:T(8,128)(2,1)S(1)}, u32[]{:S(2)}, u32[]{:S(2)}) collective-permute-start(bf16[256,128]{1,0:T(8,128)(2,1)} %param.16), channel_id=1, source_target_pairs={{0,8},{8,16},{16,24},{24,32},{32,40},{40,48},{48,56},{56,64},{64,7... | collective-permute-start | bytes 196616 | tf_op jit(solution)/shard_map/ppermute | solution.py:16
  24.3 9.1 %collective-permute-start.4 = (bf16[256,128]{1,0:T(8,128)(2,1)}, bf16[256,128]{1,0:T(8,128)(2,1)S(1)}, u32[]{:S(2)}, u32[]{:S(2)}) collective-permute-start(bf16[256,128]{1,0:T(8,128)(2,1)} %param.17), channel_id=1, source_target_pairs={{0,32},{8,40},{16,48},{24,56},{32,64},{40,72},{48,80},{56,88},{64,... | collective-permute-start | bytes 196616 | tf_op jit(solution)/shard_map/ppermute | solution.py:16
  29.3 25.9 %copy-start.3 = (bf16[256,256]{1,0:T(8,128)(2,1)S(1)}, bf16[256,256]{1,0:T(8,128)(2,1)}, u32[]{:S(2)}) copy-start(bf16[256,256]{1,0:T(8,128)(2,1)} %param.15) | copy-start | bytes 393220
  33.3 7.4 %collective-permute-start.5 = (bf16[256,128]{1,0:T(8,128)(2,1)S(1)}, bf16[256,128]{1,0:T(8,128)(2,1)S(1)}, u32[]{:S(2)}, u32[]{:S(2)}) collective-permute-start(bf16[256,128]{1,0:T(8,128)(2,1)S(1)} %copy-done.5), channel_id=1, source_target_pairs={{0,24},{8,32},{16,40},{24,48},{32,56},{40,64},{48,72},{56,80},{64,... | collective-permute-start | bytes 196616 | tf_op jit(solution)/shard_map/ppermute | solution.py:16
  40.7 7.7 %collective-permute-start.6 = (bf16[256,128]{1,0:T(8,128)(2,1)S(1)}, bf16[256,128]{1,0:T(8,128)(2,1)S(1)}, u32[]{:S(2)}, u32[]{:S(2)}) collective-permute-start(bf16[256,128]{1,0:T(8,128)(2,1)S(1)} %copy-done.5), channel_id=1, source_target_pairs={{0,16},{8,24},{16,32},{24,40},{32,48},{40,56},{48,64},{56,72},{64,... | collective-permute-start | bytes 196616 | tf_op jit(solution)/shard_map/ppermute | solution.py:16
  48.4 6.1 %collective-permute-start.7 = (bf16[256,128]{1,0:T(8,128)(2,1)S(1)}, bf16[256,128]{1,0:T(8,128)(2,1)S(1)}, u32[]{:S(2)}, u32[]{:S(2)}) collective-permute-start(bf16[256,128]{1,0:T(8,128)(2,1)S(1)} %copy-done.5), channel_id=1, source_target_pairs={{0,8},{8,16},{16,24},{24,32},{32,40},{40,48},{48,56},{56,64},{64,7... | collective-permute-start | bytes 196616 | tf_op jit(solution)/shard_map/ppermute | solution.py:16
  87.5 3.4 %copy-start.2 = (f32[1,2,256,1280]{2,3,1,0:T(8,128)S(1)}, f32[1,2,256,1280]{2,3,1,0:T(8,128)}, u32[]{:S(2)}) copy-start(f32[1,2,256,1280]{2,3,1,0:T(8,128)} %copy-done.1) | copy-start | bytes 7864324
  87.5 3.4 %copy-start.8 = (bf16[1280,128]{1,0:T(8,128)(2,1)S(1)}, bf16[1280,128]{1,0:T(8,128)(2,1)}, u32[]{:S(2)}) copy-start(bf16[1280,128]{1,0:T(8,128)(2,1)} %copy-done.7) | copy-start | bytes 983044
  87.5 3.4 %copy-start.9 = (bf16[256,256]{1,0:T(8,128)(2,1)S(1)}, bf16[256,256]{1,0:T(8,128)(2,1)}, u32[]{:S(2)}) copy-start(bf16[256,256]{1,0:T(8,128)(2,1)} %reduce-scatter.2.cloned.1.call-done) | copy-start | bytes 393220
  93.9 18.4 %collective-permute-start.12 = (bf16[256,128]{0,1:T(8,128)(2,1)}, bf16[256,128]{0,1:T(8,128)(2,1)}, u32[]{:S(2)}, u32[]{:S(2)}) collective-permute-start(bf16[256,128]{0,1:T(8,128)(2,1)} %get-tuple-element.46), channel_id=1, source_target_pairs={{8,0},{16,8},{24,16},{32,24},{40,32},{48,40},{56,48},{64,56},{72,6... | collective-permute-start | bytes 196616 | tf_op jit(solution)/shard_map/ppermute | solution.py:16
  96.1 18.2 %collective-permute-start.15 = (bf16[256,128]{0,1:T(8,128)(2,1)}, bf16[256,128]{0,1:T(8,128)(2,1)}, u32[]{:S(2)}, u32[]{:S(2)}) collective-permute-start(bf16[256,128]{0,1:T(8,128)(2,1)} %get-tuple-element.47), channel_id=1, source_target_pairs={{32,0},{40,8},{48,16},{56,24},{64,32},{72,40},{80,48},{88,56},{96,... | collective-permute-start | bytes 196616 | tf_op jit(solution)/shard_map/ppermute | solution.py:16
  100.9 21.7 %collective-permute-start.14 = (bf16[256,128]{0,1:T(8,128)(2,1)}, bf16[256,128]{0,1:T(8,128)(2,1)}, u32[]{:S(2)}, u32[]{:S(2)}) collective-permute-start(bf16[256,128]{0,1:T(8,128)(2,1)} %get-tuple-element.48), channel_id=1, source_target_pairs={{24,0},{32,8},{40,16},{48,24},{56,32},{64,40},{72,48},{80,56},{88,... | collective-permute-start | bytes 196616 | tf_op jit(solution)/shard_map/ppermute | solution.py:16
  106.1 18.5 %collective-permute-start.13 = (bf16[256,128]{0,1:T(8,128)(2,1)}, bf16[256,128]{0,1:T(8,128)(2,1)}, u32[]{:S(2)}, u32[]{:S(2)}) collective-permute-start(bf16[256,128]{0,1:T(8,128)(2,1)} %get-tuple-element.49), channel_id=1, source_target_pairs={{16,0},{24,8},{32,16},{40,24},{48,32},{56,40},{64,48},{72,56},{80,... | collective-permute-start | bytes 196616 | tf_op jit(solution)/shard_map/ppermute | solution.py:16
  109.5 16.9 %collective-permute-start.8 = (bf16[256,128]{1,0:T(8,128)(2,1)}, bf16[256,128]{1,0:T(8,128)(2,1)S(1)}, u32[]{:S(2)}, u32[]{:S(2)}) collective-permute-start(bf16[256,128]{1,0:T(8,128)(2,1)} %get-tuple-element.50), channel_id=1, source_target_pairs={{8,0},{16,8},{24,16},{32,24},{40,32},{48,40},{56,48},{64,56},{72,6... | collective-permute-start | bytes 196616 | tf_op jit(solution)/shard_map/ppermute | solution.py:16
  112.4 14.0 %collective-permute-start.11 = (bf16[256,128]{1,0:T(8,128)(2,1)}, bf16[256,128]{1,0:T(8,128)(2,1)}, u32[]{:S(2)}, u32[]{:S(2)}) collective-permute-start(bf16[256,128]{1,0:T(8,128)(2,1)} %get-tuple-element.51), channel_id=1, source_target_pairs={{32,0},{40,8},{48,16},{56,24},{64,32},{72,40},{80,48},{88,56},{96,... | collective-permute-start | bytes 196616 | tf_op jit(solution)/shard_map/ppermute | solution.py:16
  114.3 12.1 %collective-permute-start.10 = (bf16[256,128]{1,0:T(8,128)(2,1)}, bf16[256,128]{1,0:T(8,128)(2,1)}, u32[]{:S(2)}, u32[]{:S(2)}) collective-permute-start(bf16[256,128]{1,0:T(8,128)(2,1)} %get-tuple-element.52), channel_id=1, source_target_pairs={{24,0},{32,8},{40,16},{48,24},{56,32},{64,40},{72,48},{80,56},{88,... | collective-permute-start | bytes 196616 | tf_op jit(solution)/shard_map/ppermute | solution.py:16
  122.7 8.9 %collective-permute-start.9 = (bf16[256,128]{1,0:T(8,128)(2,1)}, bf16[256,128]{1,0:T(8,128)(2,1)}, u32[]{:S(2)}, u32[]{:S(2)}) collective-permute-start(bf16[256,128]{1,0:T(8,128)(2,1)} %get-tuple-element.53), channel_id=1, source_target_pairs={{16,0},{24,8},{32,16},{40,24},{48,32},{56,40},{64,48},{72,56},{80,... | collective-permute-start | bytes 196616 | tf_op jit(solution)/shard_map/ppermute | solution.py:16
  (3 other events, 3.3 us)
Sparse Core Ops, SparseCore 0:
  29.5 58.0 reduce-scatter.1
where the time goes:
time: 141 us; the launch traced here: 140 us
  starting transfers between devices  55 us (39%)
  waiting for transfers between devices  53.1 us (38%)
  between operations  14.4 us (10%)
  matrix products  8.45 us (6%)
  local copies, waits for them, and re-layouts  5.14 us (4%)
  other arithmetic  3.94 us (3%)
    ppermute x16, starting transfers between devices, shifted(): lax.ppermute(value, axis, [(source, source + steps) for source in range(l...  54.9 us
    reduce_scatter x1, waiting for transfers between devices, local(): lax.psum_scatter(lax.dot_general(out_weight, layer_cotangent, (((1,), (1,...  29.9 us
    ppermute x16, waiting for transfers between devices, shifted(): lax.ppermute(value, axis, [(source, source + steps) for source in range(l...  23.2 us
    unnamed x30, local copies, waits for them, and re-layouts  3.72 us
    dot_general x1, matrix products, local(): jnp.einsum('hgqk,hgdq->khd', probs_low, grads_four, preferred_element_typ...  3.42 us
    dot_general x1, matrix products, local(): lax.dot_general(out_weight, layer_cotangent, (((1,), (1,)), ((), ())), pr...  3.03 us
  transfers between devices with their start and end apart: 17, of which 6 were waited for; matrix products, arithmetic and copies ran while one was open for 5% of the time, Pallas kernels for 0%

commit v1 on v0

v1 whole, which is shorter than its diff:
```python
import jax
import jax.numpy as jnp
from jax import lax
from jax.experimental import pallas as pl
from jax.experimental.pallas import tpu as pltpu
from jax.sharding import PartitionSpec as P

HEAD_SIZE = 128
Y = 4
score_scale = 168.0 ** (-0.5)
MESH = pl.DeviceIdType.MESH
F32 = jnp.float32
BF16 = jnp.bfloat16


def dot(a, b, ca, cb):
    return lax.dot_general(a, b, (((ca,), (cb,)), ((), ())), preferred_element_type=F32)


def make_kernel(n_ctx, n_tp, t):
    n_u = n_tp // 2
    back = 4
    h = HEAD_SIZE
    order = (2, 1, 3, 0)

    def kernel(
        cot_hbm, w_hbm, q_hbm, k_hbm, v_hbm,
        dq_ref, dk_ref, dv_ref,
        cot, w, q_in, q2, kv, kt,
        pair_send, pair_recv, own_part, ring_send, s1_recv, d_recv, c_recv, grads,
        probs, probs_low, dprobs, dscores,
        g_send, g_recv, z_send, z_recv, g_own,
        load_sem, kvz_sem, kvy_sem, pair_sem, s1_sem, d_sem, c_sem, gk_sem, gv_sem, z_sem,
    ):
        c = lax.axis_index("ctx")
        tp = lax.axis_index("tp")
        u = tp // 2
        a = tp % 2
        y = c % Y
        plane = c - y

        loads = [
            pltpu.make_async_copy(k_hbm, kv.at[back, 0], load_sem.at[0]),
            pltpu.make_async_copy(v_hbm, kv.at[back, 1], load_sem.at[1]),
            pltpu.make_async_copy(cot_hbm, cot, load_sem.at[2]),
            pltpu.make_async_copy(w_hbm, w, load_sem.at[3]),
            pltpu.make_async_copy(q_hbm, q_in, load_sem.at[4]),
        ]
        for load in loads:
            load.start()

        following = ((c + back) % n_ctx, tp)
        preceding = ((c + n_ctx - back) % n_ctx, tp)
        other_core = (c, u * 2 + (1 - a))
        up = (c, (tp + 2) % n_tp)
        down = (c, (tp + n_tp - 2) % n_tp)

        def along(r):
            return (plane + (y + r) % Y, tp)

        barrier = pltpu.get_barrier_semaphore()
        partners = [following, preceding, other_core, up, down, along(1), along(2), along(3)]
        for partner in partners:
            pl.semaphore_signal(barrier, inc=1, device_id=partner, device_id_type=MESH)

        def remote(src, dst, sems, index, device):
            return pltpu.make_async_remote_copy(
                src_ref=src, dst_ref=dst, send_sem=sems.at[0, index], recv_sem=sems.at[1, index],
                device_id=device, device_id_type=MESH,
            )

        loads[0].wait()
        loads[1].wait()
        pl.semaphore_wait(barrier, len(partners))

        kvz = remote(kv.at[back], kv.at[0], kvz_sem, 0, following)
        kvz.start()

        loads[2].wait()
        loads[3].wait()

        def part(du, core):
            dest = ((u + du) % n_u) * 2 + core
            rows = w[pl.ds(pl.multiple_of(dest * 2 * h, 2 * h), 2 * h), :]
            return dot(cot[...], rows, 1, 1)

        pairs = []
        for i, du in enumerate(order):
            term = part(du, 1 - a)
            pair_send[i, 0:t] = term[:, :h].astype(BF16)
            pair_send[i, t:] = term[:, h:].astype(BF16)
            copy = remote(pair_send.at[i], pair_recv.at[i], pair_sem, i, other_core)
            copy.start()
            pairs.append(copy)

        s1 = [
            remote(ring_send.at[0, 0], s1_recv.at[0], s1_sem, 0, up),
            remote(ring_send.at[0, 1], s1_recv.at[1], s1_sem, 1, down),
        ]
        direct = [
            remote(ring_send.at[1, 1], d_recv.at[0], d_sem, 0, up),
            remote(ring_send.at[2, 0], d_recv.at[1], d_sem, 1, down),
        ]
        combined = [
            remote(ring_send.at[1, 0], c_recv.at[0], c_sem, 0, up),
            remote(ring_send.at[2, 1], c_recv.at[1], c_sem, 1, down),
        ]
        for i, du in enumerate(order):
            term = part(du, a)
            pairs[i].wait_recv()
            low = term[:, :h] + pair_recv[i, 0:t].astype(F32)
            high = term[:, h:] + pair_recv[i, t:].astype(F32)
            if i == 0:
                ring_send[0, 0] = low.astype(BF16)
                ring_send[0, 1] = high.astype(BF16)
                s1[0].start()
                s1[1].start()
            elif i == 1:
                ring_send[1, 1] = high.astype(BF16)
                direct[0].start()
                own_part[0] = low
            elif i == 2:
                ring_send[2, 0] = low.astype(BF16)
                direct[1].start()
                own_part[1] = high
            else:
                own_part[2] = low
                own_part[3] = high

        kvz.wait_recv()
        kvy = []
        for r in (2, 1, 3):
            source = jnp.where(y < r, back, 0)
            copy = remote(kv.at[source], kv.at[r], kvy_sem, r - 1, along(Y - r))
            copy.start()
            kvy.append(copy)

        s1[0].wait_recv()
        ring_send[1, 0] = (own_part[0] + s1_recv[0].astype(F32)).astype(BF16)
        combined[0].start()
        s1[1].wait_recv()
        ring_send[2, 1] = (own_part[1] + s1_recv[1].astype(F32)).astype(BF16)
        combined[1].start()

        loads[4].wait()
        q2[0:t] = q_in[:, :h]
        q2[t:] = q_in[:, h:]

        key_row = lax.broadcasted_iota(jnp.int32, (t, 2 * t), 0)
        query_col = lax.broadcasted_iota(jnp.int32, (t, 2 * t), 1) % t
        top = jnp.full((1, 2 * t), -jnp.inf, F32)
        for slot in (4, 0, 2, 1, 3):
            if slot in (1, 2, 3):
                kvy[(2, 1, 3).index(slot)].wait_recv()
            scores = dot(kv[slot, 0], q2[...], 1, 1) * score_scale
            here = c + slot >= back
            if slot == back:
                scores = jnp.where(key_row <= query_col, scores, -jnp.inf)
            elif slot == 0:
                scores = jnp.where((key_row > query_col) & here, scores, -jnp.inf)
            else:
                scores = jnp.where(here, scores, -jnp.inf)
            probs[slot] = scores
            top = jnp.maximum(top, jnp.max(scores, axis=0, keepdims=True))
            kt[slot] = kv[slot, 0].T
        total = jnp.zeros((1, 2 * t), F32)
        for slot in range(back + 1):
            expo = jnp.exp(probs[slot] - top)
            probs[slot] = expo
            total = total + jnp.sum(expo, axis=0, keepdims=True)
        inverse = 1.0 / total
        for slot in range(back + 1):
            prob = probs[slot] * inverse
            probs[slot] = prob
            probs_low[slot] = prob.astype(BF16)

        direct[0].wait_recv()
        direct[1].wait_recv()
        combined[0].wait_recv()
        combined[1].wait_recv()
        grads[0:t] = (
            own_part[2] + d_recv[1].astype(F32) + c_recv[0].astype(F32)
        ).astype(BF16)
        grads[t:] = (
            own_part[3] + d_recv[0].astype(F32) + c_recv[1].astype(F32)
        ).astype(BF16)

        gk, gv = {}, {}
        for r in (2, 1, 3):
            gv[r] = remote(g_send.at[r - 1, 1], g_recv.at[r - 1, 1], gv_sem, r - 1, along(r))
            gk[r] = remote(g_send.at[r - 1, 0], g_recv.at[r - 1, 0], gk_sem, r - 1, along(r))
            g_send[r - 1, 1] = dot(probs_low[r], grads[...], 1, 0).astype(BF16)
            gv[r].start()
        delta = jnp.zeros((1, 2 * t), F32)
        for slot in range(back + 1):
            dp = dot(kv[slot, 1], grads[...], 1, 1)
            dprobs[slot] = dp
            delta = delta + jnp.sum(probs[slot] * dp, axis=0, keepdims=True)
        for slot in (2, 1, 3, 0, 4):
            ds = (probs[slot] * (dprobs[slot] - delta) * score_scale).astype(BF16)
            dscores[slot] = ds
            key_part = dot(ds, q2[...], 1, 0)
            if slot in (1, 2, 3):
                g_send[slot - 1, 0] = key_part.astype(BF16)
                gk[slot].start()
            else:
                g_own[slot // 4, 0] = key_part
                g_own[slot // 4, 1] = dot(probs_low[slot], grads[...], 1, 0)
        turned = jnp.zeros((h, 2 * t), F32)
        for slot in range(back + 1):
            turned = turned + dot(kt[slot], dscores[slot], 1, 0)
        dq_ref[:, :h] = turned[:, :t].T.astype(BF16)
        dq_ref[:, h:] = turned[:, t:].T.astype(BF16)

        for part_index, copies in ((1, gv), (0, gk)):
            for r in (2, 1, 3):
                copies[r].wait_recv()
                arrived = g_recv[r - 1, part_index].astype(F32)
                earlier = y >= r
                g_own[0, part_index] += jnp.where(earlier, arrived, 0.0)
                g_own[1, part_index] += jnp.where(earlier, 0.0, arrived)
        z_send[...] = g_own[0].astype(BF16)
        last = remote(z_send, z_recv, z_sem, 0, preceding)
        last.start()
        last.wait_recv()
        dk_ref[...] = (g_own[1, 0] + z_recv[0].astype(F32)).astype(BF16)
        dv_ref[...] = (g_own[1, 1] + z_recv[1].astype(F32)).astype(BF16)

        for copy in [kvz, *kvy, *pairs, *s1, *direct, *combined, *gk.values(), *gv.values(), last]:
            copy.wait_send()

    return kernel


def solution(mesh):
    n_ctx, n_tp = mesh.shape["ctx"], mesh.shape["tp"]

    def local(layer_cotangent, out_weight, queries, keys, values):
        t, d = layer_cotangent.shape
        h = HEAD_SIZE
        vmem = pltpu.VMEM
        dma = pltpu.SemaphoreType.DMA
        scratch = [
            vmem((t, d), BF16),
            vmem(out_weight.shape, BF16),
            vmem((t, 2 * h), BF16),
            vmem((2 * t, h), BF16),
            vmem((5, 2, t, h), BF16),
            vmem((5, h, t), BF16),
            vmem((4, 2 * t, h), BF16),
            vmem((4, 2 * t, h), BF16),
            vmem((4, t, h), F32),
            vmem((3, 2, t, h), BF16),
            vmem((2, t, h), BF16),
            vmem((2, t, h), BF16),
            vmem((2, t, h), BF16),
            vmem((2 * t, h), BF16),
            vmem((5, t, 2 * t), F32),
            vmem((5, t, 2 * t), BF16),
            vmem((5, t, 2 * t), F32),
            vmem((5, t, 2 * t), BF16),
            vmem((3, 2, t, h), BF16),
            vmem((3, 2, t, h), BF16),
            vmem((2, t, h), BF16),
            vmem((2, t, h), BF16),
            vmem((2, 2, t, h), F32),
            dma((5,)),
            dma((2, 1)),
            dma((2, 3)),
            dma((2, 4)),
            dma((2, 2)),
            dma((2, 2)),
            dma((2, 2)),
            dma((2, 3)),
            dma((2, 3)),
            dma((2, 1)),
        ]
        return pl.pallas_call(
            make_kernel(n_ctx, n_tp, t),
            out_shape=(
                jax.ShapeDtypeStruct(queries.shape, BF16),
                jax.ShapeDtypeStruct(keys.shape, BF16),
                jax.ShapeDtypeStruct(values.shape, BF16),
            ),
            in_specs=[pl.BlockSpec(memory_space=pl.ANY)] * 5,
            out_specs=tuple(pl.BlockSpec(memory_space=pltpu.VMEM) for _ in range(3)),
            scratch_shapes=scratch,
            compiler_params=pltpu.CompilerParams(
                collective_id=0, has_side_effects=True, vmem_limit_bytes=48 << 20
            ),
            name="attention_backward",
        )(layer_cotangent, out_weight, queries, keys, values)

    in_specs = (P("ctx", "tp"), P(None, "tp"), P("ctx", "tp"), P("ctx", "tp"), P("ctx", "tp"))
    out_specs = (P("ctx", "tp"), P("ctx", "tp"), P("ctx", "tp"))
    return jax.shard_map(local, mesh=mesh, in_specs=in_specs, out_specs=out_specs, check_vma=False)
```

time: 141 us -> 61.2 us (0.43)
  the two profiles are of different devices: /device:TPU:26 before, /device:TPU:2 now
where the time goes in v1:
time: 61.2 us; the launch traced here: 60.8 us
  Pallas kernels  51.4 us (84%)
  local copies, waits for them, and re-layouts  8.75 us (14%)
  between operations  0.66 us (1%)
    pallas_call x1, Pallas kernels, local(): pl.pallas_call(make_kernel(n_ctx, n_tp, t), out_shape=(jax.ShapeDtypeStru...  51.4 us
    unnamed x11, local copies, waits for them, and re-layouts  8.75 us

profile of v1, /device:TPU:2, one launch (start us, length us, event | category | flops | bytes accessed | tf_op | source)
XLA Modules:
  0.0 60.8 jit_solution(8303641258847535565)
XLA Ops:
  0.6 1.1 %copy.8.cot_hbm = bf16[256,672]{1,0:T(8,128)(2,1)S(1)} copy(bf16[256,672]{0,1:T(8,128)(2,1)} %param.5) | data formatting | bytes 688128 | tf_op args[0]
  1.8 3.1 %copy.9.w_hbm = bf16[2048,672]{1,0:T(8,128)(2,1)S(1)} copy(bf16[2048,672]{0,1:T(8,128)(2,1)} %param.6) | data formatting | bytes 5505024 | tf_op args[1]
  4.9 0.0 copy-start
  4.9 0.9 %copy-done = bf16[256,256]{1,0:T(8,128)(2,1)S(1)} copy-done((bf16[256,256]{1,0:T(8,128)(2,1)S(1)}, bf16[256,256]{1,0:T(8,128)(2,1)}, u32[]{:S(2)}) %copy-start) | copy-done | bytes 131096
  5.8 0.0 copy-start.1
  5.8 0.8 %copy-done.1 = bf16[256,128]{1,0:T(8,128)(2,1)S(1)} copy-done((bf16[256,128]{1,0:T(8,128)(2,1)S(1)}, bf16[256,128]{1,0:T(8,128)(2,1)}, u32[]{:S(2)}) %copy-start.1) | copy-done | bytes 65560
  6.6 0.0 copy-start.2
  6.7 0.8 %copy-done.2 = bf16[256,128]{1,0:T(8,128)(2,1)S(1)} copy-done((bf16[256,128]{1,0:T(8,128)(2,1)S(1)}, bf16[256,128]{1,0:T(8,128)(2,1)}, u32[]{:S(2)}) %copy-start.2) | copy-done | bytes 65560
  7.5 51.4 %attention_backward.1 = (bf16[256,256]{1,0:T(8,128)(2,1)S(1)}, bf16[256,128]{1,0:T(8,128)(2,1)S(1)}, bf16[256,128]{1,0:T(8,128)(2,1)S(1)}) custom-call(bf16[256,672]{1,0:T(8,128)(2,1)S(1)} %copy.8.cot_hbm, bf16[2048,672]{1,0:T(8,128)(2,1)S(1)} %copy.9.w_hbm, bf16[256,256]{1,0:T(8,128)(2,1)S(1)} %copy-done, bf16[256,128]{1,0:T(8,128)(2,1)S(1)} %copy-done.1, ...), custom_call_target="tpu_custom_call" | custom-call | tf_op jit(solution)/shard_map/attention_backward/pallas_call | solution.py:278
  58.9 0.7 %copy.13 = bf16[256,256]{1,0:T(8,128)(2,1)} copy(bf16[256,256]{1,0:T(8,128)(2,1)S(1)} %get-tuple-element.6) | data formatting | bytes 262144
  59.6 0.6 %copy.14 = bf16[256,128]{1,0:T(8,128)(2,1)} copy(bf16[256,128]{1,0:T(8,128)(2,1)S(1)} %get-tuple-element.7) | data formatting | bytes 131072
  60.2 0.6 %copy.15 = bf16[256,128]{1,0:T(8,128)(2,1)} copy(bf16[256,128]{1,0:T(8,128)(2,1)S(1)} %get-tuple-element.8) | data formatting | bytes 131072
Async XLA Ops:
  4.9 0.9 %copy-start = (bf16[256,256]{1,0:T(8,128)(2,1)S(1)}, bf16[256,256]{1,0:T(8,128)(2,1)}, u32[]{:S(2)}) copy-start(bf16[256,256]{1,0:T(8,128)(2,1)} %q_hbm.1) | copy-start | bytes 393220
  5.8 0.8 %copy-start.1 = (bf16[256,128]{1,0:T(8,128)(2,1)S(1)}, bf16[256,128]{1,0:T(8,128)(2,1)}, u32[]{:S(2)}) copy-start(bf16[256,128]{1,0:T(8,128)(2,1)} %k_hbm.1) | copy-start | bytes 196612
  6.6 0.8 %copy-start.2 = (bf16[256,128]{1,0:T(8,128)(2,1)S(1)}, bf16[256,128]{1,0:T(8,128)(2,1)}, u32[]{:S(2)}) copy-start(bf16[256,128]{1,0:T(8,128)(2,1)} %v_hbm.1) | copy-start | bytes 196612

commit v2 on v1

--- a/solution.py
+++ b/solution.py
@@ -17,6 +17,15 @@
     return lax.dot_general(a, b, (((ca,), (cb,)), ((), ())), preferred_element_type=F32)
 
 
+def write_out(dq_in, dk_in, dv_in, dq_out, dk_out, dv_out, sem):
+    pairs = ((dq_in, dq_out), (dk_in, dk_out), (dv_in, dv_out))
+    copies = [pltpu.make_async_copy(a, b, sem.at[i]) for i, (a, b) in enumerate(pairs)]
+    for copy in copies:
+        copy.start()
+    for copy in copies:
+        copy.wait()
+
+
 def make_kernel(n_ctx, n_tp, t):
     n_u = n_tp // 2
     back = 4
@@ -26,8 +35,8 @@
     def kernel(
         cot_hbm, w_hbm, q_hbm, k_hbm, v_hbm,
         dq_ref, dk_ref, dv_ref,
-        cot, w, q_in, q2, kv, kt,
-        pair_send, pair_recv, own_part, ring_send, s1_recv, d_recv, c_recv, grads,
+        cot_turned, cot, w, q_in, q2, kv, kt,
+        pair_send, pair_recv, own_terms, own_part, ring_send, s1_recv, d_recv, c_recv, grads,
         probs, probs_low, dprobs, dscores,
         g_send, g_recv, z_send, z_recv, g_own,
         load_sem, kvz_sem, kvy_sem, pair_sem, s1_sem, d_sem, c_sem, gk_sem, gv_sem, z_sem,
@@ -42,7 +51,7 @@
         loads = [
             pltpu.make_async_copy(k_hbm, kv.at[back, 0], load_sem.at[0]),
             pltpu.make_async_copy(v_hbm, kv.at[back, 1], load_sem.at[1]),
-            pltpu.make_async_copy(cot_hbm, cot, load_sem.at[2]),
+            pltpu.make_async_copy(cot_hbm, cot_turned, load_sem.at[2]),
             pltpu.make_async_copy(w_hbm, w, load_sem.at[3]),
             pltpu.make_async_copy(q_hbm, q_in, load_sem.at[4]),
         ]
@@ -77,22 +86,33 @@
         kvz.start()
 
         loads[2].wait()
+        cot[...] = cot_turned[...].T
         loads[3].wait()
 
         def part(du, core):
             dest = ((u + du) % n_u) * 2 + core
-            rows = w[pl.ds(pl.multiple_of(dest * 2 * h, 2 * h), 2 * h), :]
-            return dot(cot[...], rows, 1, 1)
+            columns = w[:, pl.ds(pl.multiple_of(dest * 2 * h, 2 * h), 2 * h)]
+            return dot(cot[...], columns, 1, 0)
 
         pairs = []
-        for i, du in enumerate(order):
-            term = part(du, 1 - a)
+
+        def for_other(i):
+            term = part(order[i], 1 - a)
             pair_send[i, 0:t] = term[:, :h].astype(BF16)
             pair_send[i, t:] = term[:, h:].astype(BF16)
             copy = remote(pair_send.at[i], pair_recv.at[i], pair_sem, i, other_core)
             copy.start()
             pairs.append(copy)
 
+        def for_this(i):
+            own_terms[i] = part(order[i], a)
+
+        def pair_sum(i):
+            pairs[i].wait_recv()
+            low = own_terms[i, :, :h] + pair_recv[i, 0:t].astype(F32)
+            high = own_terms[i, :, h:] + pair_recv[i, t:].astype(F32)
+            return low, high
+
         s1 = [
             remote(ring_send.at[0, 0], s1_recv.at[0], s1_sem, 0, up),
             remote(ring_send.at[0, 1], s1_recv.at[1], s1_sem, 1, down),
@@ -105,27 +125,28 @@
             remote(ring_send.at[1, 0], c_recv.at[0], c_sem, 0, up),
             remote(ring_send.at[2, 1], c_recv.at[1], c_sem, 1, down),
         ]
-        for i, du in enumerate(order):
-            term = part(du, a)
-            pairs[i].wait_recv()
-            low = term[:, :h] + pair_recv[i, 0:t].astype(F32)
-            high = term[:, h:] + pair_recv[i, t:].astype(F32)
-            if i == 0:
-                ring_send[0, 0] = low.astype(BF16)
-                ring_send[0, 1] = high.astype(BF16)
-                s1[0].start()
-                s1[1].start()
-            elif i == 1:
-                ring_send[1, 1] = high.astype(BF16)
-                direct[0].start()
-                own_part[0] = low
-            elif i == 2:
-                ring_send[2, 0] = low.astype(BF16)
-                direct[1].start()
-                own_part[1] = high
-            else:
-                own_part[2] = low
-                own_part[3] = high
+        for_other(0)
+        for_this(0)
+        for_other(1)
+        for_other(2)
+        low, high = pair_sum(0)
+        ring_send[0, 0] = low.astype(BF16)
+        ring_send[0, 1] = high.astype(BF16)
+        s1[0].start()
+        s1[1].start()
+        for_other(3)
+        for_this(1)
+        for_this(2)
+        for_this(3)
+        low, high = pair_sum(1)
+        ring_send[1, 1] = high.astype(BF16)
+        own_part[0] = low
+        low, high = pair_sum(2)
+        ring_send[2, 0] = low.astype(BF16)
+        own_part[1] = high
+        low, high = pair_sum(3)
+        own_part[2] = low
+        own_part[3] = high
 
         kvz.wait_recv()
         kvy = []
@@ -135,6 +156,10 @@
             copy.start()
             kvy.append(copy)
 
+        s1[0].wait_send()
+        direct[0].start()
+        s1[1].wait_send()
+        direct[1].start()
         s1[0].wait_recv()
         ring_send[1, 0] = (own_part[0] + s1_recv[0].astype(F32)).astype(BF16)
         combined[0].start()
@@ -196,37 +221,45 @@
             dp = dot(kv[slot, 1], grads[...], 1, 1)
             dprobs[slot] = dp
             delta = delta + jnp.sum(probs[slot] * dp, axis=0, keepdims=True)
-        for slot in (2, 1, 3, 0, 4):
+        for slot in (2, 1, 3):
             ds = (probs[slot] * (dprobs[slot] - delta) * score_scale).astype(BF16)
             dscores[slot] = ds
-            key_part = dot(ds, q2[...], 1, 0)
-            if slot in (1, 2, 3):
-                g_send[slot - 1, 0] = key_part.astype(BF16)
-                gk[slot].start()
-            else:
-                g_own[slot // 4, 0] = key_part
-                g_own[slot // 4, 1] = dot(probs_low[slot], grads[...], 1, 0)
+            g_send[slot - 1, 0] = dot(ds, q2[...], 1, 0).astype(BF16)
+            gk[slot].start()
+        for slot in (0, 4):
+            g_own[slot // 4, 1] = dot(probs_low[slot], grads[...], 1, 0)
+        for slot in (0, 4):
+            ds = (probs[slot] * (dprobs[slot] - delta) * score_scale).astype(BF16)
+            dscores[slot] = ds
+            g_own[slot // 4, 0] = dot(ds, q2[...], 1, 0)
+
+        z_copies = [
+            remote(z_send.at[i], z_recv.at[i], z_sem, i, preceding) for i in range(2)
+        ]
+
+        def gather(i, copies):
+            for r in (1, 3, 2):
+                copies[r].wait_recv()
+                arrived = g_recv[r - 1, i].astype(F32)
+                earlier = y >= r
+                g_own[0, i] += jnp.where(earlier, arrived, 0.0)
+                g_own[1, i] += jnp.where(earlier, 0.0, arrived)
+            z_send[i] = g_own[0, i].astype(BF16)
+            z_copies[i].start()
+
+        gather(1, gv)
         turned = jnp.zeros((h, 2 * t), F32)
         for slot in range(back + 1):
             turned = turned + dot(kt[slot], dscores[slot], 1, 0)
         dq_ref[:, :h] = turned[:, :t].T.astype(BF16)
         dq_ref[:, h:] = turned[:, t:].T.astype(BF16)
-
-        for part_index, copies in ((1, gv), (0, gk)):
-            for r in (2, 1, 3):
-                copies[r].wait_recv()
-                arrived = g_recv[r - 1, part_index].astype(F32)
-                earlier = y >= r
-                g_own[0, part_index] += jnp.where(earlier, arrived, 0.0)
-                g_own[1, part_index] += jnp.where(earlier, 0.0, arrived)
-        z_send[...] = g_own[0].astype(BF16)
-        last = remote(z_send, z_recv, z_sem, 0, preceding)
-        last.start()
-        last.wait_recv()
+        gather(0, gk)
+        z_copies[1].wait_recv()
+        dv_ref[...] = (g_own[1, 1] + z_recv[1].astype(F32)).astype(BF16)
+        z_copies[0].wait_recv()
         dk_ref[...] = (g_own[1, 0] + z_recv[0].astype(F32)).astype(BF16)
-        dv_ref[...] = (g_own[1, 1] + z_recv[1].astype(F32)).astype(BF16)
-
-        for copy in [kvz, *kvy, *pairs, *s1, *direct, *combined, *gk.values(), *gv.values(), last]:
+
+        for copy in [kvz, *kvy, *pairs, *direct, *combined, *gk.values(), *gv.values(), *z_copies]:
             copy.wait_send()
 
     return kernel
@@ -241,14 +274,16 @@
         vmem = pltpu.VMEM
         dma = pltpu.SemaphoreType.DMA
         scratch = [
+            vmem((d, t), BF16),
             vmem((t, d), BF16),
-            vmem(out_weight.shape, BF16),
+            vmem(out_weight.shape[::-1], BF16),
             vmem((t, 2 * h), BF16),
             vmem((2 * t, h), BF16),
             vmem((5, 2, t, h), BF16),
             vmem((5, h, t), BF16),
             vmem((4, 2 * t, h), BF16),
             vmem((4, 2 * t, h), BF16),
+            vmem((4, t, 2 * h), F32),
             vmem((4, t, h), F32),
             vmem((3, 2, t, h), BF16),
             vmem((2, t, h), BF16),
@@ -273,23 +308,32 @@
             dma((2, 2)),
             dma((2, 3)),
             dma((2, 3)),
-            dma((2, 1)),
-        ]
-        return pl.pallas_call(
+            dma((2, 2)),
+        ]
+        outs = pl.pallas_call(
             make_kernel(n_ctx, n_tp, t),
             out_shape=(
                 jax.ShapeDtypeStruct(queries.shape, BF16),
                 jax.ShapeDtypeStruct(keys.shape, BF16),
                 jax.ShapeDtypeStruct(values.shape, BF16),
             ),
-            in_specs=[pl.BlockSpec(memory_space=pl.ANY)] * 5,
+            in_specs=[pl.BlockSpec(memory_space=pltpu.HBM)] * 5,
             out_specs=tuple(pl.BlockSpec(memory_space=pltpu.VMEM) for _ in range(3)),
             scratch_shapes=scratch,
             compiler_params=pltpu.CompilerParams(
                 collective_id=0, has_side_effects=True, vmem_limit_bytes=48 << 20
             ),
             name="attention_backward",
-        )(layer_cotangent, out_weight, queries, keys, values)
+        )(*(pltpu.with_memory_space_constraint(x, pltpu.HBM) for x in (layer_cotangent.T, out_weight.T, queries, keys, values)))
+        return pl.pallas_call(
+            write_out,
+            out_shape=tuple(jax.ShapeDtypeStruct(o.shape, o.dtype) for o in outs),
+            in_specs=[pl.BlockSpec(memory_space=pltpu.VMEM)] * 3,
+            out_specs=tuple(pl.BlockSpec(memory_space=pl.ANY) for _ in outs),
+            scratch_shapes=[dma((3,))],
+            compiler_params=pltpu.CompilerParams(vmem_limit_bytes=4 << 20),
+            name="write_out",
+        )(*outs)
 
     in_specs = (P("ctx", "tp"), P(None, "tp"), P("ctx", "tp"), P("ctx", "tp"), P("ctx", "tp"))
     out_specs = (P("ctx", "tp"), P("ctx", "tp"), P("ctx", "tp"))

time: 61.2 us -> 52 us (0.85)
  local copies, waits for them, and re-layouts: 8.75 us -> 0 us
    unnamed x11 -> x0, local copies, waits for them, and re-layouts: 8.75 us -> none
    pallas_call x1, Pallas kernels: 51.4 us -> 50.6 us  [local(): pl.pallas_call(make_kernel(n_ctx, n_tp, t), out_shape=(jax.ShapeDtypeStru...]
    pallas_call x0 -> x1, Pallas kernels: none -> 0.72 us  [local(): pl.pallas_call(write_out, out_shape=tuple((jax.ShapeDtypeStruct(o.shape,...]
where the time goes in v2:
time: 52 us; the launch traced here: 51.9 us
  Pallas kernels  51.3 us (99%)
  between operations  0.64 us (1%)
    pallas_call x1, Pallas kernels, local(): pl.pallas_call(make_kernel(n_ctx, n_tp, t), out_shape=(jax.ShapeDtypeStru...  50.6 us

profile of v2, /device:TPU:2, one launch (start us, length us, event | category | flops | bytes accessed | tf_op | source)
XLA Modules:
  0.0 51.9 jit_solution(10190457346245517797)
XLA Ops:
  0.6 50.6 %attention_backward.1 = (bf16[256,256]{1,0:T(8,128)(2,1)S(1)}, bf16[256,128]{1,0:T(8,128)(2,1)S(1)}, bf16[256,128]{1,0:T(8,128)(2,1)S(1)}) custom-call(bf16[672,256]{1,0:T(8,128)(2,1)} %bitcast.3, bf16[672,2048]{1,0:T(8,128)(2,1)} %bitcast.2, bf16[256,256]{1,0:T(8,128)(2,1)} %q_hbm.1, bf16[256,128]{1,0:T(8,128)(2,1)} %k_hbm.1, bf16[256,128]{1,0:T(8,128)(2,1)} %v_hbm.1), custom_call_target="tpu_custom_call" | custom-call | tf_op jit(solution)/shard_map/attention_backward/pallas_call | solution.py:313
  51.2 0.7 %write_out.1 = (bf16[256,256]{1,0:T(8,128)(2,1)}, bf16[256,128]{1,0:T(8,128)(2,1)}, bf16[256,128]{1,0:T(8,128)(2,1)}) custom-call(bf16[256,256]{1,0:T(8,128)(2,1)S(1)} %get-tuple-element.6.dq_in, bf16[256,128]{1,0:T(8,128)(2,1)S(1)} %get-tuple-element.7.dk_in, bf16[256,128]{1,0:T(8,128)(2,1)S(1)} %get-tuple-element.8.dv_in), custom_call_target="tpu_custom_call" | custom-call | tf_op jit(solution)/shard_map/write_out/pallas_call | solution.py:328

commit v3 on v2

--- a/solution.py
+++ b/solution.py
@@ -39,7 +39,7 @@
         pair_send, pair_recv, own_terms, own_part, ring_send, s1_recv, d_recv, c_recv, grads,
         probs, probs_low, dprobs, dscores,
         g_send, g_recv, z_send, z_recv, g_own,
-        load_sem, kvz_sem, kvy_sem, pair_sem, s1_sem, d_sem, c_sem, gk_sem, gv_sem, z_sem,
+        load_sem, kvz_sem, kvy_sem, pair_sem, s1_sem, d_sem, c_sem, gk_sem, gv_sem, z_sem, turn_sem,
     ):
         c = lax.axis_index("ctx")
         tp = lax.axis_index("tp")
@@ -52,11 +52,13 @@
             pltpu.make_async_copy(k_hbm, kv.at[back, 0], load_sem.at[0]),
             pltpu.make_async_copy(v_hbm, kv.at[back, 1], load_sem.at[1]),
             pltpu.make_async_copy(cot_hbm, cot_turned, load_sem.at[2]),
-            pltpu.make_async_copy(w_hbm, w, load_sem.at[3]),
-            pltpu.make_async_copy(q_hbm, q_in, load_sem.at[4]),
-        ]
-        for load in loads:
-            load.start()
+        ]
+        for i, du in enumerate(order):
+            columns = pl.ds(pl.multiple_of(((u + du) % n_u) * 4 * h, 4 * h), 4 * h)
+            loads.append(pltpu.make_async_copy(w_hbm.at[:, columns], w.at[:, columns], load_sem.at[3 + i]))
+        loads.append(pltpu.make_async_copy(q_hbm, q_in, load_sem.at[7]))
+        loads[2].start()
+        loads[3].start()
 
         following = ((c + back) % n_ctx, tp)
         preceding = ((c + n_ctx - back) % n_ctx, tp)
@@ -72,23 +74,15 @@
         for partner in partners:
             pl.semaphore_signal(barrier, inc=1, device_id=partner, device_id_type=MESH)
 
+        loads[0].start()
+        loads[1].start()
+
         def remote(src, dst, sems, index, device):
             return pltpu.make_async_remote_copy(
                 src_ref=src, dst_ref=dst, send_sem=sems.at[0, index], recv_sem=sems.at[1, index],
                 device_id=device, device_id_type=MESH,
             )
 
-        loads[0].wait()
-        loads[1].wait()
-        pl.semaphore_wait(barrier, len(partners))
-
-        kvz = remote(kv.at[back], kv.at[0], kvz_sem, 0, following)
-        kvz.start()
-
-        loads[2].wait()
-        cot[...] = cot_turned[...].T
-        loads[3].wait()
-
         def part(du, core):
             dest = ((u + du) % n_u) * 2 + core
             columns = w[:, pl.ds(pl.multiple_of(dest * 2 * h, 2 * h), 2 * h)]
@@ -97,12 +91,11 @@
         pairs = []
 
         def for_other(i):
+            loads[3 + i].wait()
             term = part(order[i], 1 - a)
             pair_send[i, 0:t] = term[:, :h].astype(BF16)
             pair_send[i, t:] = term[:, h:].astype(BF16)
-            copy = remote(pair_send.at[i], pair_recv.at[i], pair_sem, i, other_core)
-            copy.start()
-            pairs.append(copy)
+            pairs.append(remote(pair_send.at[i], pair_recv.at[i], pair_sem, i, other_core))
 
         def for_this(i):
             own_terms[i] = part(order[i], a)
@@ -125,16 +118,33 @@
             remote(ring_send.at[1, 0], c_recv.at[0], c_sem, 0, up),
             remote(ring_send.at[2, 1], c_recv.at[1], c_sem, 1, down),
         ]
+        loads[2].wait()
+        cot[...] = cot_turned[...].T
+        for load in loads[4:]:
+            load.start()
         for_other(0)
         for_this(0)
+        pl.semaphore_wait(barrier, len(partners))
+        pairs[0].start()
+        loads[0].wait()
+        loads[1].wait()
+        kvz = remote(kv.at[back], kv.at[0], kvz_sem, 0, following)
+        kvz.start()
         for_other(1)
         for_other(2)
         low, high = pair_sum(0)
         ring_send[0, 0] = low.astype(BF16)
         ring_send[0, 1] = high.astype(BF16)
-        s1[0].start()
-        s1[1].start()
+
+        @pl.when(a == 0)
+        def _():
+            s1[0].start()
+            s1[1].start()
+
+        pairs[1].start()
+        pairs[2].start()
         for_other(3)
+        pairs[3].start()
         for_this(1)
         for_this(2)
         for_this(3)
@@ -148,6 +158,14 @@
         own_part[2] = low
         own_part[3] = high
 
+        @pl.when(a == 0)
+        def _():
+            s1[0].wait_send()
+            s1[1].wait_send()
+            pl.semaphore_signal(turn_sem, inc=1, device_id=other_core, device_id_type=MESH)
+            direct[0].start()
+            direct[1].start()
+
         kvz.wait_recv()
         kvy = []
         for r in (2, 1, 3):
@@ -156,10 +174,16 @@
             copy.start()
             kvy.append(copy)
 
-        s1[0].wait_send()
-        direct[0].start()
-        s1[1].wait_send()
-        direct[1].start()
+        @pl.when(a == 1)
+        def _():
+            pl.semaphore_wait(turn_sem, 1)
+            s1[0].start()
+            s1[1].start()
+            s1[0].wait_send()
+            direct[0].start()
+            s1[1].wait_send()
+            direct[1].start()
+
         s1[0].wait_recv()
         ring_send[1, 0] = (own_part[0] + s1_recv[0].astype(F32)).astype(BF16)
         combined[0].start()
@@ -167,7 +191,7 @@
         ring_send[2, 1] = (own_part[1] + s1_recv[1].astype(F32)).astype(BF16)
         combined[1].start()
 
-        loads[4].wait()
+        loads[7].wait()
         q2[0:t] = q_in[:, :h]
         q2[t:] = q_in[:, h:]
 
@@ -211,7 +235,7 @@
         ).astype(BF16)
 
         gk, gv = {}, {}
-        for r in (2, 1, 3):
+        for r in (1, 2, 3):
             gv[r] = remote(g_send.at[r - 1, 1], g_recv.at[r - 1, 1], gv_sem, r - 1, along(r))
             gk[r] = remote(g_send.at[r - 1, 0], g_recv.at[r - 1, 0], gk_sem, r - 1, along(r))
             g_send[r - 1, 1] = dot(probs_low[r], grads[...], 1, 0).astype(BF16)
@@ -221,7 +245,7 @@
             dp = dot(kv[slot, 1], grads[...], 1, 1)
             dprobs[slot] = dp
             delta = delta + jnp.sum(probs[slot] * dp, axis=0, keepdims=True)
-        for slot in (2, 1, 3):
+        for slot in (1, 2, 3):
             ds = (probs[slot] * (dprobs[slot] - delta) * score_scale).astype(BF16)
             dscores[slot] = ds
             g_send[slot - 1, 0] = dot(ds, q2[...], 1, 0).astype(BF16)
@@ -237,30 +261,37 @@
             remote(z_send.at[i], z_recv.at[i], z_sem, i, preceding) for i in range(2)
         ]
 
-        def gather(i, copies):
-            for r in (1, 3, 2):
-                copies[r].wait_recv()
-                arrived = g_recv[r - 1, i].astype(F32)
-                earlier = y >= r
-                g_own[0, i] += jnp.where(earlier, arrived, 0.0)
-                g_own[1, i] += jnp.where(earlier, 0.0, arrived)
+        def add(i, copies, into):
+            for r in (1, 2, 3):
+                @pl.when((y >= r) if into == 0 else (y < r))
+                def _():
+                    copies[r].wait_recv()
+                    g_own[into, i] += g_recv[r - 1, i].astype(F32)
+
+        def pass_on(i, copies):
+            add(i, copies, 0)
             z_send[i] = g_own[0, i].astype(BF16)
             z_copies[i].start()
 
-        gather(1, gv)
+        pass_on(1, gv)
         turned = jnp.zeros((h, 2 * t), F32)
         for slot in range(back + 1):
             turned = turned + dot(kt[slot], dscores[slot], 1, 0)
         dq_ref[:, :h] = turned[:, :t].T.astype(BF16)
         dq_ref[:, h:] = turned[:, t:].T.astype(BF16)
-        gather(0, gk)
+        pass_on(0, gk)
+        add(1, gv, 1)
+        add(0, gk, 1)
         z_copies[1].wait_recv()
         dv_ref[...] = (g_own[1, 1] + z_recv[1].astype(F32)).astype(BF16)
         z_copies[0].wait_recv()
         dk_ref[...] = (g_own[1, 0] + z_recv[0].astype(F32)).astype(BF16)
 
-        for copy in [kvz, *kvy, *pairs, *direct, *combined, *gk.values(), *gv.values(), *z_copies]:
+        for copy in [kvz, *kvy, *pairs, *combined, *gk.values(), *gv.values(), *z_copies]:
             copy.wait_send()
+
+        direct[0].wait_send()
+        direct[1].wait_send()
 
     return kernel
 
@@ -299,7 +330,7 @@
             vmem((2, t, h), BF16),
             vmem((2, t, h), BF16),
             vmem((2, 2, t, h), F32),
-            dma((5,)),
+            dma((8,)),
             dma((2, 1)),
             dma((2, 3)),
             dma((2, 4)),
@@ -309,6 +340,7 @@
             dma((2, 3)),
             dma((2, 3)),
             dma((2, 2)),
+            pltpu.SemaphoreType.REGULAR,
         ]
         outs = pl.pallas_call(
             make_kernel(n_ctx, n_tp, t),

time: 52 us -> 48 us (0.923)
  the two profiles are of different devices: /device:TPU:2 before, /device:TPU:19 now
where the time goes in v3:
time: 48 us; the launch traced here: 47.8 us
  Pallas kernels  47.2 us (98%)
  between operations  0.64 us (1%)
    pallas_call x1, Pallas kernels, local(): pl.pallas_call(make_kernel(n_ctx, n_tp, t), out_shape=(jax.ShapeDtypeStru...  46.5 us

profile of v3, /device:TPU:19, one launch (start us, length us, event | category | flops | bytes accessed | tf_op | source)
XLA Modules:
  0.0 47.8 jit_solution(3883777115311002253)
XLA Ops:
  0.6 46.5 %attention_backward.1 = (bf16[256,256]{1,0:T(8,128)(2,1)S(1)}, bf16[256,128]{1,0:T(8,128)(2,1)S(1)}, bf16[256,128]{1,0:T(8,128)(2,1)S(1)}) custom-call(bf16[672,256]{1,0:T(8,128)(2,1)} %bitcast.3, bf16[672,2048]{1,0:T(8,128)(2,1)} %bitcast.2, bf16[256,256]{1,0:T(8,128)(2,1)} %q_hbm.1, bf16[256,128]{1,0:T(8,128)(2,1)} %k_hbm.1, bf16[256,128]{1,0:T(8,128)(2,1)} %v_hbm.1), custom_call_target="tpu_custom_call" | custom-call | tf_op jit(solution)/shard_map/attention_backward/pallas_call | solution.py:345
  47.1 0.7 %write_out.1 = (bf16[256,256]{1,0:T(8,128)(2,1)}, bf16[256,128]{1,0:T(8,128)(2,1)}, bf16[256,128]{1,0:T(8,128)(2,1)}) custom-call(bf16[256,256]{1,0:T(8,128)(2,1)S(1)} %get-tuple-element.6.dq_in, bf16[256,128]{1,0:T(8,128)(2,1)S(1)} %get-tuple-element.7.dk_in, bf16[256,128]{1,0:T(8,128)(2,1)S(1)} %get-tuple-element.8.dv_in), custom_call_target="tpu_custom_call" | custom-call | tf_op jit(solution)/shard_map/write_out/pallas_call | solution.py:360

commit v4 on v3

--- a/solution.py
+++ b/solution.py
@@ -37,7 +37,7 @@
         dq_ref, dk_ref, dv_ref,
         cot_turned, cot, w, q_in, q2, kv, kt,
         pair_send, pair_recv, own_terms, own_part, ring_send, s1_recv, d_recv, c_recv, grads,
-        probs, probs_low, dprobs, dscores,
+        probs, probs_low, dscores, vt, mixed_values, grads_turned,
         g_send, g_recv, z_send, z_recv, g_own,
         load_sem, kvz_sem, kvy_sem, pair_sem, s1_sem, d_sem, c_sem, gk_sem, gv_sem, z_sem, turn_sem,
     ):
@@ -57,9 +57,6 @@
             columns = pl.ds(pl.multiple_of(((u + du) % n_u) * 4 * h, 4 * h), 4 * h)
             loads.append(pltpu.make_async_copy(w_hbm.at[:, columns], w.at[:, columns], load_sem.at[3 + i]))
         loads.append(pltpu.make_async_copy(q_hbm, q_in, load_sem.at[7]))
-        loads[2].start()
-        loads[3].start()
-
         following = ((c + back) % n_ctx, tp)
         preceding = ((c + n_ctx - back) % n_ctx, tp)
         other_core = (c, u * 2 + (1 - a))
@@ -70,12 +67,12 @@
             return (plane + (y + r) % Y, tp)
 
         barrier = pltpu.get_barrier_semaphore()
-        partners = [following, preceding, other_core, up, down, along(1), along(2), along(3)]
+        partners = [up, down, following, preceding, along(2), along(1), along(3), other_core]
         for partner in partners:
             pl.semaphore_signal(barrier, inc=1, device_id=partner, device_id_type=MESH)
 
-        loads[0].start()
-        loads[1].start()
+        for i in (2, 3, 0, 1):
+            loads[i].start()
 
         def remote(src, dst, sems, index, device):
             return pltpu.make_async_remote_copy(
@@ -212,50 +209,59 @@
             probs[slot] = scores
             top = jnp.maximum(top, jnp.max(scores, axis=0, keepdims=True))
             kt[slot] = kv[slot, 0].T
+            vt[slot] = kv[slot, 1].T
         total = jnp.zeros((1, 2 * t), F32)
         for slot in range(back + 1):
             expo = jnp.exp(probs[slot] - top)
             probs[slot] = expo
             total = total + jnp.sum(expo, axis=0, keepdims=True)
         inverse = 1.0 / total
+        mixed = jnp.zeros((h, 2 * t), F32)
         for slot in range(back + 1):
             prob = probs[slot] * inverse
-            probs[slot] = prob
-            probs_low[slot] = prob.astype(BF16)
+            probs[slot] = prob * score_scale
+            rough = prob.astype(BF16)
+            probs_low[slot] = rough
+            rest = (prob - rough.astype(F32)).astype(BF16)
+            mixed = mixed + dot(vt[slot], rough, 1, 0) + dot(vt[slot], rest, 1, 0)
+        mixed_values[...] = mixed
 
         direct[0].wait_recv()
         direct[1].wait_recv()
         combined[0].wait_recv()
         combined[1].wait_recv()
-        grads[0:t] = (
-            own_part[2] + d_recv[1].astype(F32) + c_recv[0].astype(F32)
-        ).astype(BF16)
-        grads[t:] = (
-            own_part[3] + d_recv[0].astype(F32) + c_recv[1].astype(F32)
-        ).astype(BF16)
+        low = (own_part[2] + d_recv[1].astype(F32) + c_recv[0].astype(F32)).astype(BF16)
+        high = (own_part[3] + d_recv[0].astype(F32) + c_recv[1].astype(F32)).astype(BF16)
+        grads[0:t] = low
+        grads[t:] = high
+        grads_turned[:, 0:t] = low.T
+        grads_turned[:, t:] = high.T
 
         gk, gv = {}, {}
         for r in (1, 2, 3):
             gv[r] = remote(g_send.at[r - 1, 1], g_recv.at[r - 1, 1], gv_sem, r - 1, along(r))
             gk[r] = remote(g_send.at[r - 1, 0], g_recv.at[r - 1, 0], gk_sem, r - 1, along(r))
-            g_send[r - 1, 1] = dot(probs_low[r], grads[...], 1, 0).astype(BF16)
+        value_parts = dot(probs_low[1:4].reshape(3 * t, 2 * t), grads[...], 1, 0)
+        for r in (1, 2, 3):
+            g_send[r - 1, 1] = value_parts[(r - 1) * t : r * t].astype(BF16)
             gv[r].start()
-        delta = jnp.zeros((1, 2 * t), F32)
-        for slot in range(back + 1):
-            dp = dot(kv[slot, 1], grads[...], 1, 1)
-            dprobs[slot] = dp
-            delta = delta + jnp.sum(probs[slot] * dp, axis=0, keepdims=True)
+        delta = jnp.sum(mixed_values[...] * grads_turned[...].astype(F32), axis=0, keepdims=True)
+
+        def score_grads(first, count):
+            slots = slice(first, first + count)
+            dp = dot(kv[slots, 1].reshape(count * t, h), grads_turned[...], 1, 0)
+            ds = probs[slots].reshape(count * t, 2 * t) * (dp - delta)
+            ds = ds.astype(BF16)
+            dscores[slots] = ds.reshape(count, t, 2 * t)
+            return ds
+
+        key_parts = dot(score_grads(1, 3), q2[...], 1, 0)
         for slot in (1, 2, 3):
-            ds = (probs[slot] * (dprobs[slot] - delta) * score_scale).astype(BF16)
-            dscores[slot] = ds
-            g_send[slot - 1, 0] = dot(ds, q2[...], 1, 0).astype(BF16)
+            g_send[slot - 1, 0] = key_parts[(slot - 1) * t : slot * t].astype(BF16)
             gk[slot].start()
         for slot in (0, 4):
             g_own[slot // 4, 1] = dot(probs_low[slot], grads[...], 1, 0)
-        for slot in (0, 4):
-            ds = (probs[slot] * (dprobs[slot] - delta) * score_scale).astype(BF16)
-            dscores[slot] = ds
-            g_own[slot // 4, 0] = dot(ds, q2[...], 1, 0)
+            g_own[slot // 4, 0] = dot(score_grads(slot, 1), q2[...], 1, 0)
 
         z_copies = [
             remote(z_send.at[i], z_recv.at[i], z_sem, i, preceding) for i in range(2)
@@ -323,8 +329,10 @@
             vmem((2 * t, h), BF16),
             vmem((5, t, 2 * t), F32),
             vmem((5, t, 2 * t), BF16),
-            vmem((5, t, 2 * t), F32),
             vmem((5, t, 2 * t), BF16),
+            vmem((5, h, t), BF16),
+            vmem((h, 2 * t), F32),
+            vmem((h, 2 * t), BF16),
             vmem((3, 2, t, h), BF16),
             vmem((3, 2, t, h), BF16),
             vmem((2, t, h), BF16),

time: 48 us -> 48.2 us (level)
  the two profiles are of different devices: /device:TPU:19 before, /device:TPU:17 now
where the time goes in v4:
time: 48.2 us; the launch traced here: 48.1 us
  Pallas kernels  47.4 us (98%)
  between operations  0.64 us (1%)
    pallas_call x1, Pallas kernels, local(): pl.pallas_call(make_kernel(n_ctx, n_tp, t), out_shape=(jax.ShapeDtypeStru...  46.7 us

profile of v4, /device:TPU:17, one launch (start us, length us, event | category | flops | bytes accessed | tf_op | source)
XLA Modules:
  0.0 48.1 jit_solution(11496661526735283073)
XLA Ops:
  0.6 46.7 %attention_backward.1 = (bf16[256,256]{1,0:T(8,128)(2,1)S(1)}, bf16[256,128]{1,0:T(8,128)(2,1)S(1)}, bf16[256,128]{1,0:T(8,128)(2,1)S(1)}) custom-call(bf16[672,256]{1,0:T(8,128)(2,1)} %bitcast.3, bf16[672,2048]{1,0:T(8,128)(2,1)} %bitcast.2, bf16[256,256]{1,0:T(8,128)(2,1)} %q_hbm.1, bf16[256,128]{1,0:T(8,128)(2,1)} %k_hbm.1, bf16[256,128]{1,0:T(8,128)(2,1)} %v_hbm.1), custom_call_target="tpu_custom_call" | custom-call | tf_op jit(solution)/shard_map/attention_backward/pallas_call | solution.py:353
  47.3 0.7 %write_out.1 = (bf16[256,256]{1,0:T(8,128)(2,1)}, bf16[256,128]{1,0:T(8,128)(2,1)}, bf16[256,128]{1,0:T(8,128)(2,1)}) custom-call(bf16[256,256]{1,0:T(8,128)(2,1)S(1)} %get-tuple-element.6.dq_in, bf16[256,128]{1,0:T(8,128)(2,1)S(1)} %get-tuple-element.7.dk_in, bf16[256,128]{1,0:T(8,128)(2,1)S(1)} %get-tuple-element.8.dv_in), custom_call_target="tpu_custom_call" | custom-call | tf_op jit(solution)/shard_map/write_out/pallas_call | solution.py:368

commit v5 on v4

--- a/solution.py
+++ b/solution.py
@@ -47,6 +47,8 @@
         a = tp % 2
         y = c % Y
         plane = c - y
+        early = (c // Y) % 4 == 1
+        yields = ((c // Y) % 4 >= 2) & (a == 1)
 
         loads = [
             pltpu.make_async_copy(k_hbm, kv.at[back, 0], load_sem.at[0]),
@@ -158,8 +160,17 @@
         @pl.when(a == 0)
         def _():
             s1[0].wait_send()
+
+            @pl.when(early)
+            def _():
+                pl.semaphore_signal(turn_sem, inc=1, device_id=other_core, device_id_type=MESH)
+
             s1[1].wait_send()
-            pl.semaphore_signal(turn_sem, inc=1, device_id=other_core, device_id_type=MESH)
+
+            @pl.when(jnp.logical_not(early))
+            def _():
+                pl.semaphore_signal(turn_sem, inc=1, device_id=other_core, device_id_type=MESH)
+
             direct[0].start()
             direct[1].start()
 
@@ -179,7 +190,11 @@
             s1[0].wait_send()
             direct[0].start()
             s1[1].wait_send()
-            direct[1].start()
+
+            @pl.when(jnp.logical_not(yields))
+            def _():
+                direct[1].start()
+
 
         s1[0].wait_recv()
         ring_send[1, 0] = (own_part[0] + s1_recv[0].astype(F32)).astype(BF16)
@@ -187,6 +202,11 @@
         s1[1].wait_recv()
         ring_send[2, 1] = (own_part[1] + s1_recv[1].astype(F32)).astype(BF16)
         combined[1].start()
+
+        @pl.when(yields)
+        def _():
+            direct[1].start()
+
 
         loads[7].wait()
         q2[0:t] = q_in[:, :h]

time: 48.2 us -> 47.1 us (0.977)
  the two profiles are of different devices: /device:TPU:17 before, /device:TPU:57 now
where the time goes in v5:
time: 47.1 us; the launch traced here: 47 us
  Pallas kernels  46.3 us (98%)
  between operations  0.64 us (1%)
    pallas_call x1, Pallas kernels, local(): pl.pallas_call(make_kernel(n_ctx, n_tp, t), out_shape=(jax.ShapeDtypeStru...  45.6 us

profile of v5, /device:TPU:57, one launch (start us, length us, event | category | flops | bytes accessed | tf_op | source)
XLA Modules:
  0.0 47.0 jit_solution(10158100697570220825)
XLA Ops:
  0.6 45.6 %attention_backward.1 = (bf16[256,256]{1,0:T(8,128)(2,1)S(1)}, bf16[256,128]{1,0:T(8,128)(2,1)S(1)}, bf16[256,128]{1,0:T(8,128)(2,1)S(1)}) custom-call(bf16[672,256]{1,0:T(8,128)(2,1)} %bitcast.3, bf16[672,2048]{1,0:T(8,128)(2,1)} %bitcast.2, bf16[256,256]{1,0:T(8,128)(2,1)} %q_hbm.1, bf16[256,128]{1,0:T(8,128)(2,1)} %k_hbm.1, bf16[256,128]{1,0:T(8,128)(2,1)} %v_hbm.1), custom_call_target="tpu_custom_call" | custom-call | tf_op jit(solution)/shard_map/attention_backward/pallas_call | solution.py:373
  46.2 0.7 %write_out.1 = (bf16[256,256]{1,0:T(8,128)(2,1)}, bf16[256,128]{1,0:T(8,128)(2,1)}, bf16[256,128]{1,0:T(8,128)(2,1)}) custom-call(bf16[256,256]{1,0:T(8,128)(2,1)S(1)} %get-tuple-element.6.dq_in, bf16[256,128]{1,0:T(8,128)(2,1)S(1)} %get-tuple-element.7.dk_in, bf16[256,128]{1,0:T(8,128)(2,1)S(1)} %get-tuple-element.8.dv_in), custom_call_target="tpu_custom_call" | custom-call | tf_op jit(solution)/shard_map/write_out/pallas_call | solution.py:388

commit v6 on v5

--- a/solution.py
+++ b/solution.py
@@ -48,7 +48,7 @@
         y = c % Y
         plane = c - y
         early = (c // Y) % 4 == 1
-        yields = ((c // Y) % 4 >= 2) & (a == 1)
+        yields = ((c // Y) % 4 == 3) & (a == 1)
 
         loads = [
             pltpu.make_async_copy(k_hbm, kv.at[back, 0], load_sem.at[0]),

time: 47.1 us -> 47.2 us (level)
  the two profiles are of different devices: /device:TPU:57 before, /device:TPU:49 now
where the time goes in v6:
time: 47.2 us; the launch traced here: 47 us
  Pallas kernels  46.4 us (98%)
  between operations  0.64 us (1%)
    pallas_call x1, Pallas kernels, local(): pl.pallas_call(make_kernel(n_ctx, n_tp, t), out_shape=(jax.ShapeDtypeStru...  45.7 us

profile of v6, /device:TPU:49, one launch (start us, length us, event | category | flops | bytes accessed | tf_op | source)
XLA Modules:
  0.0 47.0 jit_solution(7785201481666635844)
XLA Ops:
  0.6 45.7 %attention_backward.1 = (bf16[256,256]{1,0:T(8,128)(2,1)S(1)}, bf16[256,128]{1,0:T(8,128)(2,1)S(1)}, bf16[256,128]{1,0:T(8,128)(2,1)S(1)}) custom-call(bf16[672,256]{1,0:T(8,128)(2,1)} %bitcast.3, bf16[672,2048]{1,0:T(8,128)(2,1)} %bitcast.2, bf16[256,256]{1,0:T(8,128)(2,1)} %q_hbm.1, bf16[256,128]{1,0:T(8,128)(2,1)} %k_hbm.1, bf16[256,128]{1,0:T(8,128)(2,1)} %v_hbm.1), custom_call_target="tpu_custom_call" | custom-call | tf_op jit(solution)/shard_map/attention_backward/pallas_call | solution.py:373
  46.3 0.7 %write_out.1 = (bf16[256,256]{1,0:T(8,128)(2,1)}, bf16[256,128]{1,0:T(8,128)(2,1)}, bf16[256,128]{1,0:T(8,128)(2,1)}) custom-call(bf16[256,256]{1,0:T(8,128)(2,1)S(1)} %get-tuple-element.6.dq_in, bf16[256,128]{1,0:T(8,128)(2,1)S(1)} %get-tuple-element.7.dk_in, bf16[256,128]{1,0:T(8,128)(2,1)S(1)} %get-tuple-element.8.dv_in), custom_call_target="tpu_custom_call" | custom-call | tf_op jit(solution)/shard_map/write_out/pallas_call | solution.py:388

commit v7 on v5

--- a/solution.py
+++ b/solution.py
@@ -279,9 +279,12 @@
         for slot in (1, 2, 3):
             g_send[slot - 1, 0] = key_parts[(slot - 1) * t : slot * t].astype(BF16)
             gk[slot].start()
-        for slot in (0, 4):
+
+        def kept(slot):
             g_own[slot // 4, 1] = dot(probs_low[slot], grads[...], 1, 0)
             g_own[slot // 4, 0] = dot(score_grads(slot, 1), q2[...], 1, 0)
+
+        kept(0)
 
         z_copies = [
             remote(z_send.at[i], z_recv.at[i], z_sem, i, preceding) for i in range(2)
@@ -300,12 +303,13 @@
             z_copies[i].start()
 
         pass_on(1, gv)
+        kept(4)
+        pass_on(0, gk)
         turned = jnp.zeros((h, 2 * t), F32)
         for slot in range(back + 1):
             turned = turned + dot(kt[slot], dscores[slot], 1, 0)
         dq_ref[:, :h] = turned[:, :t].T.astype(BF16)
         dq_ref[:, h:] = turned[:, t:].T.astype(BF16)
-        pass_on(0, gk)
         add(1, gv, 1)
         add(0, gk, 1)
         z_copies[1].wait_recv()

time: 47.1 us -> 47.1 us (level)
  no operation moved by 1% of the time
where the time goes in v7:
time: 47.1 us; the launch traced here: 46.9 us
  Pallas kernels  46.3 us (98%)
  between operations  0.64 us (1%)
    pallas_call x1, Pallas kernels, local(): pl.pallas_call(make_kernel(n_ctx, n_tp, t), out_shape=(jax.ShapeDtypeStru...  45.5 us

profile of v7, /device:TPU:57, one launch (start us, length us, event | category | flops | bytes accessed | tf_op | source)
XLA Modules:
  0.0 46.9 jit_solution(13670901930309483984)
XLA Ops:
  0.6 45.5 %attention_backward.1 = (bf16[256,256]{1,0:T(8,128)(2,1)S(1)}, bf16[256,128]{1,0:T(8,128)(2,1)S(1)}, bf16[256,128]{1,0:T(8,128)(2,1)S(1)}) custom-call(bf16[672,256]{1,0:T(8,128)(2,1)} %bitcast.3, bf16[672,2048]{1,0:T(8,128)(2,1)} %bitcast.2, bf16[256,256]{1,0:T(8,128)(2,1)} %q_hbm.1, bf16[256,128]{1,0:T(8,128)(2,1)} %k_hbm.1, bf16[256,128]{1,0:T(8,128)(2,1)} %v_hbm.1), custom_call_target="tpu_custom_call" | custom-call | tf_op jit(solution)/shard_map/attention_backward/pallas_call | solution.py:377
  46.2 0.7 %write_out.1 = (bf16[256,256]{1,0:T(8,128)(2,1)}, bf16[256,128]{1,0:T(8,128)(2,1)}, bf16[256,128]{1,0:T(8,128)(2,1)}) custom-call(bf16[256,256]{1,0:T(8,128)(2,1)S(1)} %get-tuple-element.6.dq_in, bf16[256,128]{1,0:T(8,128)(2,1)S(1)} %get-tuple-element.7.dk_in, bf16[256,128]{1,0:T(8,128)(2,1)S(1)} %get-tuple-element.8.dv_in), custom_call_target="tpu_custom_call" | custom-call | tf_op jit(solution)/shard_map/write_out/pallas_call | solution.py:392
